TPU v7x, 256 devices: a whole 4x4x8 slice. The times are simulated.
256 devices in a mesh: cell: 32 (over y, z), lt: 8 (over x, core).
Axes of the slice: x: 4, y: 4, z: 8, core: 2. Of those that a mesh axis runs over, the one named last changes fastest.
Arguments:
- field: float32 [8, 80, 1048576], P('lt', None, 'cell'), may hold values from -54 to 54
- level_start: float32 [80, 24], replicated, may hold values from -6 to 6
- time_start: float32 [8, 6], replicated, may hold values from -6 to 6
Outputs:
- core: float32 [6, 24, 1048576], P(None, 'lt', 'cell')
- level_basis: float32 [80, 24], replicated
- time_basis: float32 [8, 6], replicated
All inputs are finite; a program needn't handle non-finite values.
Results may differ from a plain program's by a relative error of at most 0.0003.
Values sent between devices are 32-bit elements; how exact they have to be, the bound alone decides.
No kernel may reach another device: no remote copies, remote signals or barrier semaphores. Data moves between devices by JAX's collectives and lax.ppermute only.
A program may use at most 64 MiB of HBM per device.

v0:
```python
import jax
import jax.numpy as jnp
from jax import lax
from jax.sharding import PartitionSpec as P

ITERS = 3
highest = lax.Precision.HIGHEST


def orthonormal(matrix):
    square = jnp.dot(matrix.T, matrix, precision=highest)
    factor = jnp.linalg.cholesky(square)
    return lax.linalg.triangular_solve(
        factor, matrix, left_side=False, lower=True, transpose_a=True
    )


def body(field, level_start, time_start):
    level_basis = orthonormal(level_start)
    for step in range(ITERS):
        projected = jnp.einsum("slc,lr->src", field, level_basis, precision=highest)
        local_term = jnp.einsum("slc,src->lr", field, projected, precision=highest)
        applied = lax.psum(local_term, ("cell", "lt"))
        level_basis = orthonormal(applied)
    reduced = jnp.einsum("lr,slc->src", level_basis, field, precision=highest)
    regrouped = lax.all_to_all(reduced, "lt", split_axis=1, concat_axis=0, tiled=True)
    time_local = jnp.einsum("src,trc->st", regrouped, regrouped, precision=highest)
    time_gram = lax.psum(time_local, ("cell", "lt"))
    time_basis = orthonormal(time_start)
    for step in range(ITERS):
        time_basis = orthonormal(jnp.dot(time_gram, time_basis, precision=highest))
    core_local = jnp.einsum("sq,src->qrc", time_basis, regrouped, precision=highest)
    return (core_local, level_basis, time_basis)


def solution(mesh):
    placed = (P("lt", None, "cell"), P(), P())
    return jax.shard_map(
        body,
        mesh=mesh,
        in_specs=placed,
        out_specs=(P(None, "lt", "cell"), P(), P()),
        check_vma=False,
    )
```

profile of v0, /device:TPU:1, one launch (start us, length us, event | category | flops | bytes accessed | tf_op | source)
XLA Modules:
  0.0 481.1 jit_solution(1306957833141414839)
XLA Ops:
  1.6 2.2 cholesky.146
  5.1 1.8 custom-call.16
  7.2 7.9 %fusion.11 = f32[24,32768]{1,0:T(8,128)S(1)} fusion(f32[80,24]{0,1:T(8,128)S(1)} %convolution_bitcast_fusion.4, f32[1,80,32768]{2,1,0:T(8,128)} %param.9), kind=kOutput, calls=%fused_computation.12 | convolution fusion | flops 754974720 | bytes 13639168 | tf_op jit(solution)/shard_map/slc,lr->src/dot_general | solution.py:21
  15.1 8.3 %fusion.17 = f32[80,24]{0,1:T(8,128)S(1)} fusion(f32[24,32768]{1,0:T(8,128)S(1)} %fusion.11, f32[1,80,32768]{2,1,0:T(8,128)S(1)} %copy-done.1), kind=kOutput, calls=%fused_computation.18 | convolution fusion | flops 754974720 | bytes 13639168 | tf_op jit(solution)/shard_map/slc,src->lr/dot_general | solution.py:22
  23.3 81.7 %psum.28 = f32[80,24]{0,1:T(8,128)S(1)} all-reduce(f32[80,24]{0,1:T(8,128)S(1)} %fusion.17), channel_id=1, replica_groups=mesh['cell'=32,'lt'=8] {'cell','lt'}, use_global_device_ids=true, to_apply=%region_2.5 | all-reduce | flops 1920 | bytes 15360 | tf_op jit(solution)/shard_map/psum | solution.py:23
  105.2 2.2 cholesky.157
  110.8 7.7 %fusion.7 = f32[24,32768]{1,0:T(8,128)S(1)} fusion(f32[80,24]{0,1:T(8,128)S(1)} %convolution_bitcast_fusion.3, f32[1,80,32768]{2,1,0:T(8,128)} %param.9), kind=kOutput, calls=%fused_computation.8 | convolution fusion | flops 754974720 | bytes 13639168 | tf_op jit(solution)/shard_map/slc,lr->src/dot_general | solution.py:21
  118.6 10.9 %fusion.20 = f32[80,24]{0,1:T(8,128)S(1)} fusion(f32[24,32768]{1,0:T(8,128)S(1)} %fusion.7, f32[1,80,32768]{2,1,0:T(8,128)} %param.9), kind=kOutput, calls=%fused_computation.19 | convolution fusion | flops 754974720 | bytes 13639168 | tf_op jit(solution)/shard_map/slc,src->lr/dot_general | solution.py:22
  129.5 73.0 %psum.29 = f32[80,24]{0,1:T(8,128)S(1)} all-reduce(f32[80,24]{0,1:T(8,128)S(1)} %fusion.20), channel_id=1, replica_groups=mesh['cell'=32,'lt'=8] {'cell','lt'}, use_global_device_ids=true, to_apply=%region_3.6 | all-reduce | flops 1920 | bytes 15360 | tf_op jit(solution)/shard_map/psum | solution.py:23
  202.7 2.2 cholesky.168
  208.3 7.7 %fusion.3 = f32[24,32768]{1,0:T(8,128)S(1)} fusion(f32[80,24]{0,1:T(8,128)S(1)} %convolution_bitcast_fusion.2, f32[1,80,32768]{2,1,0:T(8,128)} %param.9), kind=kOutput, calls=%fused_computation.4 | convolution fusion | flops 754974720 | bytes 13639168 | tf_op jit(solution)/shard_map/slc,lr->src/dot_general | solution.py:21
  216.0 10.9 %fusion.23 = f32[80,24]{0,1:T(8,128)S(1)} fusion(f32[24,32768]{1,0:T(8,128)S(1)} %fusion.3, f32[1,80,32768]{2,1,0:T(8,128)} %param.9), kind=kOutput, calls=%fused_computation.20 | convolution fusion | flops 754974720 | bytes 13639168 | tf_op jit(solution)/shard_map/slc,src->lr/dot_general | solution.py:22
  226.9 74.1 %psum.30 = f32[80,24]{0,1:T(8,128)S(1)} all-reduce(f32[80,24]{0,1:T(8,128)S(1)} %fusion.23), channel_id=1, replica_groups=mesh['cell'=32,'lt'=8] {'cell','lt'}, use_global_device_ids=true, to_apply=%region_4.7 | all-reduce | flops 1920 | bytes 15360 | tf_op jit(solution)/shard_map/psum | solution.py:23
  301.2 2.2 cholesky.179
  306.8 7.8 %convolution_bitcast_fusion = f32[1,24,32768]{2,1,0:T(8,128)S(1)} fusion(f32[80,24]{0,1:T(8,128)S(1)} %convolution_bitcast_fusion.1, f32[1,80,32768]{2,1,0:T(8,128)} %param.9), kind=kOutput, calls=%fused_computation | convolution fusion | flops 754974720 | bytes 13639168 | tf_op jit(solution)/shard_map/lr,slc->src/dot_general | solution.py:25
  314.6 4.9 %copy.44 = f32[1,24,32768]{2,0,1:T(1,128)} copy(f32[1,24,32768]{2,1,0:T(8,128)S(1)} %convolution_bitcast_fusion) | data formatting | bytes 6291456 | tf_op jit(solution)/shard_map/lr,slc->src/transpose | solution.py:25
  319.5 5.6 %all-to-all-start = ((f32[1,24,32768]{2,0,1:T(1,128)}), f32[1,24,32768]{2,0,1:T(1,128)}, u32[]{:S(2)}, u32[]{:S(2)}) async-start(f32[1,24,32768]{2,0,1:T(1,128)} %copy.44), calls=%async_computation | async-start | bytes 6291456 | tf_op jit(solution)/shard_map/all_to_all | solution.py:26
  327.9 34.3 %all-to-all-done = f32[1,24,32768]{2,0,1:T(1,128)} async-done(((f32[1,24,32768]{2,0,1:T(1,128)}), f32[1,24,32768]{2,0,1:T(1,128)}, u32[]{:S(2)}, u32[]{:S(2)}) %all-to-all-start) | async-done | bytes 3145760 | tf_op jit(solution)/shard_map/all_to_all | solution.py:26
  362.2 9.9 %reduce.8 = f32[24,32768]{1,0:T(8,128)S(1)} reduce(f32[1,24,32768]{2,0,1:T(1,128)} %all-to-all-done, f32[]{:T(128)} %constant.59), dimensions={0}, to_apply=%all_to_all.4.reduce_sub_computation | reduce | bytes 6291460 | tf_op jit(solution)/shard_map/all_to_all | solution.py:26
  372.1 3.3 all_to_all.10
  375.4 12.4 %fusion.26 = f32[8,8]{1,0:T(8,128)S(1)} fusion(f32[8,3,32768]{2,1,0:T(4,128)} %all_to_all.10), kind=kOutput, calls=%fused_computation.25 | convolution fusion | flops 75497472 | bytes 3145984 | tf_op jit(solution)/shard_map/src,trc->st/dot_general | solution.py:27
  387.9 73.7 %psum.31 = f32[8,8]{1,0:T(8,128)S(1)} all-reduce(f32[8,8]{1,0:T(8,128)S(1)} %fusion.26), channel_id=1, replica_groups=mesh['cell'=32,'lt'=8] {'cell','lt'}, use_global_device_ids=true, to_apply=%region_5.8 | all-reduce | flops 64 | bytes 512 | tf_op jit(solution)/shard_map/psum | solution.py:28
  470.5 6.4 %fusion.13 = f32[6,3,32768]{2,0,1:T(8,128)S(1)} fusion(f32[8,3,32768]{2,1,0:T(4,128)} %all_to_all.10, f32[6,8]{1,0:T(8,128)S(1)} %fusion.51), kind=kOutput, calls=%fused_computation.14 | convolution fusion | flops 56623104 | bytes 5505216 | tf_op jit(solution)/shard_map/sq,src->qrc/dot_general | solution.py:32
  477.0 3.3 copy.56
  (79 shorter events, 25.7 us)
Async XLA Ops:
  0.6 0.7 copy-start
  7.2 7.9 %copy-start.1 = (f32[1,80,32768]{2,1,0:T(8,128)S(1)}, f32[1,80,32768]{2,1,0:T(8,128)}, u32[]{:S(2)}) copy-start(f32[1,80,32768]{2,1,0:T(8,128)} %param.9) | copy-start | bytes 31457284
  306.8 7.8 %copy-start.2 = (f32[80,24]{0,1:T(8,128)}, f32[80,24]{0,1:T(8,128)S(1)}, u32[]{:S(2)}) copy-start(f32[80,24]{0,1:T(8,128)S(1)} %convolution_bitcast_fusion.1) | copy-start | bytes 23044
  319.5 5.6 %copy-start.3 = (f32[8,6]{1,0:T(8,128)S(1)}, f32[8,6]{1,0:T(8,128)}, u32[]{:S(2)}) copy-start(f32[8,6]{1,0:T(8,128)} %param.11) | copy-start | bytes 580
  319.5 42.7 %all-to-all-start = ((f32[1,24,32768]{2,0,1:T(1,128)}), f32[1,24,32768]{2,0,1:T(1,128)}, u32[]{:S(2)}, u32[]{:S(2)}) async-start(f32[1,24,32768]{2,0,1:T(1,128)} %copy.44), calls=%async_computation | async-start | bytes 6291456 | tf_op jit(solution)/shard_map/all_to_all | solution.py:26
where the time goes:
time: 490 us; the launch traced here: 481 us
  blocking collectives  302 us (62%)
  matrix products  83.4 us (17%)
  other arithmetic  40.8 us (8%)
  waiting for transfers between devices  34.3 us (7%)
  local copies, waits for them, and re-layouts  13.6 us (3%)
  starting transfers between devices  5.56 us (1%)
    psum x3, blocking collectives, body(): applied = lax.psum(local_term, ('cell', 'lt'))  229 us
    psum x1, blocking collectives, body(): time_gram = lax.psum(time_local, ('cell', 'lt'))  73.7 us
    all_to_all x1, waiting for transfers between devices, body(): lax.all_to_all(reduced, 'lt', split_axis=1, concat_axis=0, tiled=True)  34.3 us
    dot_general x3, matrix products, body(): local_term = jnp.einsum('slc,src->lr', field, projected, precision=highest)  30 us
    dot_general x3, matrix products, body(): projected = jnp.einsum('slc,lr->src', field, level_basis, precision=highest)  23.4 us
    another operation x24, other arithmetic, orthonormal(): factor = jnp.linalg.cholesky(square)  16.4 us
    another operation x16, other arithmetic, orthonormal(): lax.linalg.triangular_solve(factor, matrix, left_side=False, lower=True,...  14.4 us
    dot_general x1, matrix products, body(): jnp.einsum('src,trc->st', regrouped, regrouped, precision=highest)  12.4 us
  transfers between devices with their start and end apart: 1, of which 1 were waited for; matrix products, arithmetic and copies ran while one was open for 1% of the time, Pallas kernels for 0%

commit v1 on v0

--- a/solution.py
+++ b/solution.py
@@ -20,7 +20,7 @@
     for step in range(ITERS):
         projected = jnp.einsum("slc,lr->src", field, level_basis, precision=highest)
         local_term = jnp.einsum("slc,src->lr", field, projected, precision=highest)
-        applied = lax.psum(local_term, ("cell", "lt"))
+        applied = jnp.sum(lax.all_gather(local_term, ("cell", "lt")), axis=0)
         level_basis = orthonormal(applied)
     reduced = jnp.einsum("lr,slc->src", level_basis, field, precision=highest)
     regrouped = lax.all_to_all(reduced, "lt", split_axis=1, concat_axis=0, tiled=True)

time: 490 us -> 602 us (1.23)
  waiting for transfers between devices: 34.3 us -> 352 us
  blocking collectives: 302 us -> 75.5 us
  between operations: 1.09 us -> 14.2 us
  other arithmetic: 40.8 us -> 47.4 us
    all_gather x0 -> x3, waiting for transfers between devices: none -> 318 us  [body(): applied = jnp.sum(lax.all_gather(local_term, ('cell', 'lt')), axis=0)]
    psum x3 -> x0, blocking collectives: 229 us -> none  [body(): applied = lax.psum(local_term, ('cell', 'lt'))]
    reduce_sum x0 -> x3, other arithmetic: none -> 6.57 us  [body(): applied = jnp.sum(lax.all_gather(local_term, ('cell', 'lt')), axis=0)]
  transfers between devices with their start and end apart: 1 -> 4, of which waited for: 1 -> 4; matrix products, arithmetic and copies ran while one was open for 1% -> 0% of each run, Pallas kernels for 0% -> 0%
where the time goes in v1:
time: 602 us; the launch traced here: 594 us
  waiting for transfers between devices  352 us (58%)
  matrix products  85.3 us (14%)
  blocking collectives  75.5 us (13%)
  other arithmetic  47.4 us (8%)
  between operations  14.2 us (2%)
  local copies, waits for them, and re-layouts  13.5 us (2%)
    all_gather x3, waiting for transfers between devices, body(): applied = jnp.sum(lax.all_gather(local_term, ('cell', 'lt')), axis=0)  318 us
    psum x1, blocking collectives, body(): time_gram = lax.psum(time_local, ('cell', 'lt'))  75.5 us
    all_to_all x1, waiting for transfers between devices, body(): lax.all_to_all(reduced, 'lt', split_axis=1, concat_axis=0, tiled=True)  34.3 us
    dot_general x3, matrix products, body(): local_term = jnp.einsum('slc,src->lr', field, projected, precision=highest)  31.9 us
    dot_general x3, matrix products, body(): projected = jnp.einsum('slc,lr->src', field, level_basis, precision=highest)  23.4 us
    another operation x24, other arithmetic, orthonormal(): factor = jnp.linalg.cholesky(square)  16.4 us
    another operation x16, other arithmetic, orthonormal(): lax.linalg.triangular_solve(factor, matrix, left_side=False, lower=True,...  14.4 us
    dot_general x1, matrix products, body(): jnp.einsum('src,trc->st', regrouped, regrouped, precision=highest)  12.4 us
  transfers between devices with their start and end apart: 4, of which 4 were waited for; matrix products, arithmetic and copies ran while one was open for 0% of the time, Pallas kernels for 0%

profile of v1, /device:TPU:1, one launch (start us, length us, event | category | flops | bytes accessed | tf_op | source)
XLA Modules:
  0.0 593.6 jit_solution(6938460275924661301)
XLA Ops:
  8.1 2.2 cholesky.146
  13.7 7.9 %fusion.11 = f32[24,32768]{1,0:T(8,128)S(1)} fusion(f32[80,24]{0,1:T(8,128)S(1)} %convolution_bitcast_fusion.4, f32[1,80,32768]{2,1,0:T(8,128)} %param.9), kind=kOutput, calls=%fused_computation.12 | convolution fusion | flops 754974720 | bytes 13639168 | tf_op jit(solution)/shard_map/slc,lr->src/dot_general | solution.py:21
  21.6 8.9 %fusion.17 = f32[1,80,24]{1,2,0:T(8,128)} fusion(f32[24,32768]{1,0:T(8,128)S(1)} %fusion.11, f32[1,80,32768]{2,1,0:T(8,128)S(1)} %copy-done.1), kind=kOutput, calls=%fused_computation.18 | convolution fusion | flops 754974720 | bytes 13639168 | tf_op jit(solution)/shard_map/slc,src->lr/dot_general | solution.py:22
  30.7 109.3 %all-gather.10.cloned.1.call-done = f32[256,80,24]{1,2,0:T(8,128)} async-done(((f32[1,80,24]{1,2,0:T(8,128)}), f32[256,80,24]{1,2,0:T(8,128)}) %all-gather.10.cloned.1.call-update) | async-done | bytes 1966096 | tf_op jit(solution)/shard_map/all_gather | solution.py:23
  140.0 2.2 reduce_sum.27
  142.4 2.2 cholesky.157
  148.0 7.7 %fusion.7 = f32[24,32768]{1,0:T(8,128)S(1)} fusion(f32[80,24]{0,1:T(8,128)S(1)} %convolution_bitcast_fusion.3, f32[1,80,32768]{2,1,0:T(8,128)} %param.9), kind=kOutput, calls=%fused_computation.8 | convolution fusion | flops 754974720 | bytes 13639168 | tf_op jit(solution)/shard_map/slc,lr->src/dot_general | solution.py:21
  155.8 11.5 %fusion.20 = f32[1,80,24]{1,2,0:T(8,128)} fusion(f32[24,32768]{1,0:T(8,128)S(1)} %fusion.7, f32[1,80,32768]{2,1,0:T(8,128)} %param.9), kind=kOutput, calls=%fused_computation.19 | convolution fusion | flops 754974720 | bytes 13639168 | tf_op jit(solution)/shard_map/slc,src->lr/dot_general | solution.py:22
  167.6 104.1 %all-gather.12.cloned.1.call-done = f32[256,80,24]{1,2,0:T(8,128)} async-done(((f32[1,80,24]{1,2,0:T(8,128)}), f32[256,80,24]{1,2,0:T(8,128)}) %all-gather.12.cloned.1.call-update) | async-done | bytes 1966096 | tf_op jit(solution)/shard_map/all_gather | solution.py:23
  274.1 2.2 cholesky.168
  279.7 7.7 %fusion.3 = f32[24,32768]{1,0:T(8,128)S(1)} fusion(f32[80,24]{0,1:T(8,128)S(1)} %convolution_bitcast_fusion.2, f32[1,80,32768]{2,1,0:T(8,128)} %param.9), kind=kOutput, calls=%fused_computation.4 | convolution fusion | flops 754974720 | bytes 13639168 | tf_op jit(solution)/shard_map/slc,lr->src/dot_general | solution.py:21
  287.4 11.5 %fusion.23 = f32[1,80,24]{1,2,0:T(8,128)} fusion(f32[24,32768]{1,0:T(8,128)S(1)} %fusion.3, f32[1,80,32768]{2,1,0:T(8,128)} %param.9), kind=kOutput, calls=%fused_computation.20 | convolution fusion | flops 754974720 | bytes 13639168 | tf_op jit(solution)/shard_map/slc,src->lr/dot_general | solution.py:22
  298.9 104.3 %all-gather.14.cloned.1.call-done = f32[256,80,24]{1,2,0:T(8,128)} async-done(((f32[1,80,24]{1,2,0:T(8,128)}), f32[256,80,24]{1,2,0:T(8,128)}) %all-gather.14.cloned.1.call-update) | async-done | bytes 1966096 | tf_op jit(solution)/shard_map/all_gather | solution.py:23
  405.7 2.2 cholesky.179
  411.3 7.8 %convolution_bitcast_fusion = f32[1,24,32768]{2,1,0:T(8,128)S(1)} fusion(f32[80,24]{0,1:T(8,128)S(1)} %convolution_bitcast_fusion.1, f32[1,80,32768]{2,1,0:T(8,128)} %param.9), kind=kOutput, calls=%fused_computation | convolution fusion | flops 754974720 | bytes 13639168 | tf_op jit(solution)/shard_map/lr,slc->src/dot_general | solution.py:25
  419.1 4.9 copy.44
  424.0 5.1 all-to-all-start
  432.0 34.3 %all-to-all-done = f32[1,24,32768]{2,0,1:T(1,128)} async-done(((f32[1,24,32768]{2,0,1:T(1,128)}), f32[1,24,32768]{2,0,1:T(1,128)}, u32[]{:S(2)}, u32[]{:S(2)}) %all-to-all-start) | async-done | bytes 3145760 | tf_op jit(solution)/shard_map/all_to_all | solution.py:26
  466.3 9.9 %reduce.11 = f32[24,32768]{1,0:T(8,128)S(1)} reduce(f32[1,24,32768]{2,0,1:T(1,128)} %all-to-all-done, f32[]{:T(128)} %constant.61), dimensions={0}, to_apply=%all_to_all.4.reduce_sub_computation | reduce | bytes 6291460 | tf_op jit(solution)/shard_map/all_to_all | solution.py:26
  476.2 3.3 all_to_all.10
  479.5 12.4 %fusion.26 = f32[8,8]{1,0:T(8,128)S(1)} fusion(f32[8,3,32768]{2,1,0:T(4,128)} %all_to_all.10), kind=kOutput, calls=%fused_computation.25 | convolution fusion | flops 75497472 | bytes 3145984 | tf_op jit(solution)/shard_map/src,trc->st/dot_general | solution.py:27
  491.9 75.5 %psum.7 = f32[8,8]{1,0:T(8,128)S(1)} all-reduce(f32[8,8]{1,0:T(8,128)S(1)} %fusion.26), channel_id=1, replica_groups=mesh['cell'=32,'lt'=8] {'cell','lt'}, use_global_device_ids=true, to_apply=%region_5.8 | all-reduce | flops 64 | bytes 512 | tf_op jit(solution)/shard_map/psum | solution.py:28
  576.5 6.4 %fusion.13 = f32[6,3,32768]{2,0,1:T(8,128)S(1)} fusion(f32[8,3,32768]{2,1,0:T(4,128)} %all_to_all.10, f32[6,8]{1,0:T(8,128)S(1)} %fusion.51), kind=kOutput, calls=%fused_computation.14 | convolution fusion | flops 56623104 | bytes 5505216 | tf_op jit(solution)/shard_map/sq,src->qrc/dot_general | solution.py:32
  582.9 3.3 copy.56
  (88 shorter events, 32.4 us)
Async XLA Ops:
  7.2 0.7 copy-start
  7.2 132.8 %all-gather.10.cloned.1.call-start = ((), (), s32[]{:S(2)}) async-start(), calls=%async_computation.1 | async-start | bytes 3158016 | tf_op jit(solution)/shard_map/all_gather | solution.py:23
  13.7 7.9 %copy-start.1 = (f32[1,80,32768]{2,1,0:T(8,128)S(1)}, f32[1,80,32768]{2,1,0:T(8,128)}, u32[]{:S(2)}) copy-start(f32[1,80,32768]{2,1,0:T(8,128)} %param.9) | copy-start | bytes 31457284
  30.5 241.1 %all-gather.12.cloned.1.call-start = ((), (), s32[]{:S(2)}) async-start(), calls=%async_computation.2 | async-start | bytes 3158016 | tf_op jit(solution)/shard_map/all_gather | solution.py:23
  167.3 236.0 %all-gather.14.cloned.1.call-start = ((), (), s32[]{:S(2)}) async-start(), calls=%async_computation.3 | async-start | bytes 3158016 | tf_op jit(solution)/shard_map/all_gather | solution.py:23
  411.3 7.8 %copy-start.2 = (f32[80,24]{0,1:T(8,128)}, f32[80,24]{0,1:T(8,128)S(1)}, u32[]{:S(2)}) copy-start(f32[80,24]{0,1:T(8,128)S(1)} %convolution_bitcast_fusion.1) | copy-start | bytes 23044
  424.0 5.2 copy-start.3
  424.0 42.3 %all-to-all-start = ((f32[1,24,32768]{2,0,1:T(1,128)}), f32[1,24,32768]{2,0,1:T(1,128)}, u32[]{:S(2)}, u32[]{:S(2)}) async-start(f32[1,24,32768]{2,0,1:T(1,128)} %copy.44), calls=%async_computation | async-start | bytes 6291456 | tf_op jit(solution)/shard_map/all_to_all | solution.py:26
Sparse Core Ops, SparseCore 0:
  30.6 109.3 all-gather.9
  167.4 104.1 all-gather.11
  299.1 104.1 all-gather.13
